TPU v7x, 32 devices: a whole 2x2x4 slice. The times are simulated.
32 devices in a mesh: groups: 1, seq: 16 (over z, y, x), section: 1, head: 2 (over core).
Axes of the slice: x: 2, y: 2, z: 4, core: 2. Of those that a mesh axis runs over, the one named last changes fastest.
Arguments:
- queries: bfloat16 [2560, 3072], P(('groups', 'seq', 'head'), 'section'), may hold values from -24 to 24
- keys: bfloat16 [2560, 3072], P(('groups', 'seq', 'head'), 'section'), may hold values from -10.5 to 10.5
- values: bfloat16 [2560, 3072], P(('groups', 'seq', 'head'), 'section'), may hold values from -6 to 6
- text_keys: bfloat16 [128, 3072], P(('groups', 'seq', 'head'), 'section'), may hold values from -10 to 10
- text_values: bfloat16 [128, 3072], P(('groups', 'seq', 'head'), 'section'), may hold values from -6 to 6
- text_length: int32 [1], P('groups'), may hold values from 32 to 128
- out_weight: bfloat16 [3072, 3072], P(None, 'section'), may hold values from -0.109375 to 0.109375
Outputs:
- projected: bfloat16 [2560, 3072], P(('groups', 'seq', 'head'), 'section')
All inputs are finite; a program needn't handle non-finite values.
Results may differ from a plain program's by a relative error of at most 0.0065.
Values may be sent and summed in bfloat16 or wider, within the bound.
A program may use at most 128 MiB of HBM per device.

v0:
```python
import jax
import jax.numpy as jnp
from jax import lax
from jax.sharding import PartitionSpec as P

HEAD_DIM = 128


def absorb(running, queries_heads, key_rows, value_rows, usable):
    key_count = key_rows.shape[0]
    head_count = queries_heads.shape[1]
    keys_heads = key_rows.reshape(key_count, head_count, HEAD_DIM)
    values_heads = value_rows.reshape(key_count, head_count, HEAD_DIM)
    scores = jnp.einsum(
        "qhd,khd->qhk", queries_heads, keys_heads, preferred_element_type=jnp.float32
    ) * HEAD_DIM ** (-0.5)
    if usable is not None:
        scores = jnp.where(usable[None, None, :], scores, -1e30)
    highest, totals, summed = running
    renewed = jnp.maximum(highest, jnp.max(scores, axis=-1))
    factor = jnp.exp(highest - renewed)
    weights = jnp.exp(scores - renewed[:, :, None])
    totals = totals * factor + jnp.sum(weights, axis=-1)
    summed = summed * factor[:, :, None] + jnp.einsum(
        "qhk,khd->qhd",
        weights.astype(jnp.bfloat16),
        values_heads,
        preferred_element_type=jnp.float32,
    )
    return (renewed, totals, summed)


def opening(query_rows, text_rows_k, text_rows_v, text_length):
    query_count = query_rows.shape[0]
    head_count = query_rows.shape[1] // HEAD_DIM
    queries_heads = query_rows.reshape(query_count, head_count, HEAD_DIM)
    running = (
        jnp.full((query_count, head_count), -1e30, jnp.float32),
        jnp.zeros((query_count, head_count), jnp.float32),
        jnp.zeros((query_count, head_count, HEAD_DIM), jnp.float32),
    )
    usable = jnp.arange(text_rows_k.shape[0]) < text_length[0]
    return (queries_heads, absorb(running, queries_heads, text_rows_k, text_rows_v, usable))


def finish(running):
    highest, totals, summed = running
    result = summed / totals[:, :, None]
    return result.reshape(result.shape[0], result.shape[1] * HEAD_DIM).astype(jnp.bfloat16)


def shards(queries, keys, values, text_keys, text_values, text_length, out_weight):
    text_full_k, text_full_v = (
        lax.all_gather(text_keys, ("seq", "head"), axis=0, tiled=True),
        lax.all_gather(text_values, ("seq", "head"), axis=0, tiled=True),
    )
    local_q, local_k, local_v = (
        lax.all_to_all(queries, "head", split_axis=1, concat_axis=0, tiled=True),
        lax.all_to_all(keys, "head", split_axis=1, concat_axis=0, tiled=True),
        lax.all_to_all(values, "head", split_axis=1, concat_axis=0, tiled=True),
    )
    columns = local_q.shape[1]
    offset = lax.axis_index("head") * columns
    text_part_k = lax.dynamic_slice_in_dim(text_full_k, offset, columns, 1)
    text_part_v = lax.dynamic_slice_in_dim(text_full_v, offset, columns, 1)
    queries_heads, running = opening(local_q, text_part_k, text_part_v, text_length)
    running = absorb(
        running,
        queries_heads,
        lax.all_gather(local_k, "seq", axis=0, tiled=True),
        lax.all_gather(local_v, "seq", axis=0, tiled=True),
        None,
    )
    attended = lax.all_to_all(finish(running), "head", split_axis=0, concat_axis=1, tiled=True)
    result = jnp.dot(
        lax.all_gather(attended, "section", axis=1, tiled=True),
        out_weight,
        preferred_element_type=jnp.float32,
    )
    return result.astype(jnp.bfloat16)


def solution(mesh):
    return jax.shard_map(
        shards,
        mesh=mesh,
        in_specs=(
            P(("groups", "seq", "head"), "section"),
            P(("groups", "seq", "head"), "section"),
            P(("groups", "seq", "head"), "section"),
            P(("groups", "seq", "head"), "section"),
            P(("groups", "seq", "head"), "section"),
            P("groups"),
            P(None, "section"),
        ),
        out_specs=P(("groups", "seq", "head"), "section"),
        check_vma=False,
    )
```

profile of v0, /device:TPU:1, one launch (start us, length us, event | category | flops | bytes accessed | tf_op | source)
XLA Modules:
  0.0 288.5 jit_solution(8747841457372171135)
XLA Ops:
  6.5 0.0 all-gather.5.cloned.1.call-start
  6.5 1.1 copy.71
  7.6 4.5 %all_to_all.70 = bf16[80,2,1536]{2,0,1:T(8,128)(2,1)} all-to-all(bf16[80,2,1536]{2,0,1:T(8,128)(2,1)S(1)} %bitcast.71), channel_id=1, replica_groups=mesh['groups'=1,'seq'=16,'section'=1,'head'=2] {'head'}, dimensions={1} | all-to-all | bytes 983040 | tf_op jit(solution)/shard_map/all_to_all | solution.py:59
  12.1 0.0 all-gather.5.cloned.1.call-update
  12.2 0.0 all-gather.7.cloned.1.call-start
  12.2 1.1 copy.70
  13.3 4.9 %all_to_all.71 = bf16[80,2,1536]{2,0,1:T(8,128)(2,1)} all-to-all(bf16[80,2,1536]{2,0,1:T(8,128)(2,1)S(1)} %bitcast.72), channel_id=1, replica_groups=mesh['groups'=1,'seq'=16,'section'=1,'head'=2] {'head'}, dimensions={1} | all-to-all | bytes 983040 | tf_op jit(solution)/shard_map/all_to_all | solution.py:60
  18.2 0.0 all-gather.7.cloned.1.call-update
  18.2 1.8 copy.72
  20.0 3.9 %all-to-all-start = ((bf16[80,2,1536]{2,0,1:T(8,128)(2,1)}), bf16[80,2,1536]{2,0,1:T(8,128)(2,1)S(1)}, u32[]{:S(2)}, u32[]{:S(2)}) async-start(bf16[80,2,1536]{2,0,1:T(8,128)(2,1)} %bitcast.62), calls=%async_computation | async-start | bytes 983040 | tf_op jit(solution)/shard_map/all_to_all | solution.py:58
  23.9 1.3 all-to-all-done
  25.2 0.3 reshape.66
  25.6 49.3 %all-gather.1 = bf16[32,4,3072]{2,1,0:T(4,128)(2,1)S(1)} all-gather(bf16[1,4,3072]{2,1,0:T(4,128)(2,1)} %bitcast.78), channel_id=1, replica_groups=mesh['groups'=1,'seq'=16,'section'=1,'head'=2] {'seq','head'}, dimensions={0}, use_global_device_ids=true | all-gather | bytes 811008 | tf_op jit(solution)/shard_map/all_gather | solution.py:55
  74.9 0.2 reshape.73
  75.1 42.9 %all-gather = bf16[32,4,3072]{2,1,0:T(4,128)(2,1)S(1)} all-gather(bf16[1,4,3072]{2,1,0:T(4,128)(2,1)} %bitcast.79), channel_id=1, replica_groups=mesh['groups'=1,'seq'=16,'section'=1,'head'=2] {'seq','head'}, dimensions={0}, use_global_device_ids=true | all-gather | bytes 811008 | tf_op jit(solution)/shard_map/all_gather | solution.py:54
  118.0 0.2 reshape.71
  118.2 0.1 constant_dynamic-slice_fusion
  118.2 0.2 copy.36
  119.1 0.2 copy.40
  119.4 0.6 fusion.26
  120.0 9.4 %all-gather.5.cloned.1.call-done = bf16[2560,1536]{1,0:T(8,128)(2,1)} async-done(((bf16[160,1536]{1,0:T(8,128)(2,1)}), bf16[2560,1536]{1,0:T(8,128)(2,1)}) %all-gather.5.cloned.1.call-update) | async-done | bytes 7864336 | tf_op jit(solution)/shard_map/all_gather | solution.py:70
  129.4 10.8 %copy.43 = bf16[2560,1536]{0,1:T(8,128)(2,1)} copy(bf16[2560,1536]{1,0:T(8,128)(2,1)} %all-gather.5.cloned.1.call-done) | data formatting | bytes 15728640 | tf_op jit(solution)/shard_map/all_gather | solution.py:70
  140.3 13.0 %bitcast_reduce_fusion = (f32[160,12]{0,1:T(8,128)S(1)}, f32[12,2560,160]{1,2,0:T(8,128)}) fusion(bf16[2560,12,128]{0,2,1:T(8,128)(2,1)} %bitcast.64, bf16[160,12,128]{2,1,0:T(8,128)(2,1)S(1)} %reshape.66), kind=kOutput, calls=%fused_computation.1 | convolution fusion | flops 1268119680 | bytes 28024320 | tf_op jit(solution)/shard_map/qhd,khd->qhk/dot_general | solution.py:14
  153.3 10.0 %fusion.1 = f32[160,12]{0,1:T(8,128)S(1)} fusion(f32[12,2560,160]{1,2,0:T(8,128)} %get-tuple-element.13, f32[160,12]{0,1:T(8,128)S(1)} %get-tuple-element.8), kind=kLoop, calls=%fused_computation.3 | loop fusion | flops 14743680 | bytes 19676160 | tf_op jit(solution)/shard_map/reduce_sum | solution.py:23
  163.3 76.6 %all-gather.7.cloned.1.call-done = bf16[2560,1536]{1,0:T(8,128)(2,1)} async-done(((bf16[160,1536]{1,0:T(8,128)(2,1)}), bf16[2560,1536]{1,0:T(8,128)(2,1)}) %all-gather.7.cloned.1.call-update) | async-done | bytes 7864336 | tf_op jit(solution)/shard_map/all_gather | solution.py:71
  239.9 10.8 %copy.47 = bf16[2560,1536]{0,1:T(8,128)(2,1)} copy(bf16[2560,1536]{1,0:T(8,128)(2,1)} %all-gather.7.cloned.1.call-done) | data formatting | bytes 15728640 | tf_op jit(solution)/shard_map/all_gather | solution.py:71
  250.7 11.6 %fusion.7 = f32[160,12,128]{2,0,1:T(8,128)S(1)} fusion(bf16[2560,12,128]{0,2,1:T(8,128)(2,1)} %bitcast.65, f32[12,2560,160]{1,2,0:T(8,128)} %get-tuple-element.13, f32[160,12]{0,1:T(8,128)S(1)} %get-tuple-element.8), kind=kOutput, calls=%fused_computation.9 | convolution fusion | flops 1273036800 | bytes 28515840 | tf_op jit(solution)/shard_map/qhk,khd->qhd/dot_general | solution.py:24
  262.4 0.8 fusion.17
  263.2 1.3 fusion.16
  264.5 0.2 copy.49
  264.7 0.3 convert_element_type.19
  265.1 6.1 %all_to_all.72 = bf16[2,80,1536]{2,1,0:T(8,128)(2,1)S(1)} all-to-all(bf16[2,80,1536]{2,1,0:T(8,128)(2,1)S(1)} %convert_element_type.19), channel_id=1, replica_groups=mesh['groups'=1,'seq'=16,'section'=1,'head'=2] {'head'}, dimensions={0} | all-to-all | bytes 983040 | tf_op jit(solution)/shard_map/all_to_all | solution.py:74
  271.2 10.5 %convolution_convert_fusion = bf16[80,3072]{1,0:T(8,128)(2,1)} fusion(bf16[80,3072]{1,0:T(8,128)(2,1)S(1)} %bitcast.66, bf16[3072,3072]{1,0:T(8,128)(2,1)} %param.13), kind=kOutput, calls=%fused_computation.8 | convolution fusion | flops 1510195200 | bytes 19857408 | tf_op jit(solution)/shard_map/dot_general | solution.py:75
  (4 shorter events, 0.1 us)
Async XLA Ops:
  6.5 122.9 %all-gather.5.cloned.1.call-start = ((), (), s32[]{:S(2)}) async-start(), calls=%async_computation.4 | async-start | bytes 8355840 | tf_op jit(solution)/shard_map/all_gather | solution.py:70
  12.2 227.7 %all-gather.7.cloned.1.call-start = ((), (), s32[]{:S(2)}) async-start(), calls=%async_computation.5 | async-start | bytes 8355840 | tf_op jit(solution)/shard_map/all_gather | solution.py:71
  20.0 5.2 %all-to-all-start = ((bf16[80,2,1536]{2,0,1:T(8,128)(2,1)}), bf16[80,2,1536]{2,0,1:T(8,128)(2,1)S(1)}, u32[]{:S(2)}, u32[]{:S(2)}) async-start(bf16[80,2,1536]{2,0,1:T(8,128)(2,1)} %bitcast.62), calls=%async_computation | async-start | bytes 983040 | tf_op jit(solution)/shard_map/all_to_all | solution.py:58
Sparse Core Ops, SparseCore 0:
  12.3 117.1 all-gather.4
  132.2 107.5 all-gather.6
where the time goes:
time: 290 us; the launch traced here: 289 us
  blocking collectives  108 us (37%)
  waiting for transfers between devices  87.4 us (30%)
  matrix products  37.1 us (13%)
  local copies, waits for them, and re-layouts  27.4 us (9%)
  between operations  14.2 us (5%)
  other arithmetic  10.8 us (4%)
  starting transfers between devices  3.91 us (1%)
    all_gather x1, waiting for transfers between devices, shards(): lax.all_gather(local_v, 'seq', axis=0, tiled=True)  76.6 us
    all_gather x1, blocking collectives, shards(): lax.all_gather(text_values, ('seq', 'head'), axis=0, tiled=True)  49.3 us
    all_gather x1, blocking collectives, shards(): lax.all_gather(text_keys, ('seq', 'head'), axis=0, tiled=True)  42.9 us
    dot_general x2, matrix products, absorb(): jnp.einsum('qhd,khd->qhk', queries_heads, keys_heads, preferred_element_t...  13.7 us
    dot_general x2, matrix products, absorb(): jnp.einsum('qhk,khd->qhd', weights.astype(jnp.bfloat16), values_heads, pr...  12.9 us
    all_gather x1, local copies, waits for them, and re-layouts, shards(): lax.all_gather(local_k, 'seq', axis=0, tiled=True)  10.8 us
    all_gather x1, local copies, waits for them, and re-layouts, shards(): lax.all_gather(local_v, 'seq', axis=0, tiled=True)  10.8 us
    reduce_sum x2, other arithmetic, absorb(): totals = totals * factor + jnp.sum(weights, axis=-1)  10.8 us
  transfers between devices with their start and end apart: 3, of which 3 were waited for; matrix products, arithmetic and copies ran while one was open for 13% of the time, Pallas kernels for 0%

commit v1 on v0

v1 whole, which is shorter than its diff:
```python
import functools
import math

import jax
import jax.numpy as jnp
import numpy as np
from jax import lax
from jax.experimental import pallas as pl
from jax.experimental.pallas import tpu as pltpu
from jax.sharding import PartitionSpec as P

HEAD_DIM = 128
PAD = 16
MESH = pl.DeviceIdType.MESH


def kernel(
    dims,
    length_ref,
    q_ref,
    k_ref,
    v_ref,
    t_ref,
    order_ref,
    pick_ref,
    w_hbm,
    o_ref,
    qb,
    kv,
    tb,
    tkv,
    ob,
    att,
    wb,
    acc,
    local_sem,
    w_sem,
    q_send,
    kv_send,
    t_send,
    o_send,
    q_recv,
    kv_recv,
    t_recv,
    o_recv,
    kv2_send,
    kv2_recv,
    t2_send,
    t2_recv,
):
    A, R, C, X, hp = dims
    d = HEAD_DIM
    rows = q_ref.shape[0]
    seq = lax.axis_index("seq")
    core = lax.axis_index("head")
    section = lax.axis_index("section")
    a = seq // R
    r = lax.rem(seq, R)
    slot = r * C + core
    width = hp * d

    def at(a2=None, r2=None, c2=None, x2=None):
        return {
            "seq": (a if a2 is None else a2) * R + (r if r2 is None else r2),
            "head": core if c2 is None else c2,
            "section": section if x2 is None else x2,
        }

    def cols(start, size):
        return pl.ds(pl.multiple_of(start, d), size)

    def own_rows(which):
        return pl.ds(pl.multiple_of(which * rows, 16), rows)

    barrier = pltpu.get_barrier_semaphore()

    def greet(target):
        pl.semaphore_signal(barrier, inc=1, device_id=target, device_id_type=MESH)

    for da in range(A):
        for dx in range(X):
            if da or dx:
                greet(at(a2=lax.rem(a + da, A), x2=lax.rem(section + dx, X)))
    for dr in range(1, R):
        greet(at(r2=lax.rem(r + dr, R)))
    for dc in range(1, C):
        greet(at(c2=lax.rem(core + dc, C)))
    pl.semaphore_wait(barrier, A * X - 1 + R - 1 + C - 1)

    def remote(src, dst, send, recv, target):
        return pltpu.make_async_remote_copy(
            src_ref=src, dst_ref=dst, send_sem=send, recv_sem=recv, device_id=target, device_id_type=MESH
        )

    def first(j, which):
        src_cols = lambda a2: cols((a2 * hp + j) * d, d)
        if which == "kv":
            pairs = ((k_ref, 0), (v_ref, 1))
            for ref, n in pairs:
                pltpu.make_async_copy(ref.at[:, src_cols(a)], kv.at[j, n, slot, own_rows(a)], kv_recv.at[j]).start()

            def one(da, _):
                a2 = lax.rem(a + da, A)
                for ref, n in pairs:
                    remote(
                        ref.at[:, src_cols(a2)], kv.at[j, n, slot, own_rows(a)], kv_send.at[j], kv_recv.at[j], at(a2=a2)
                    ).start()
                return 0

            lax.fori_loop(1, A, one, 0)
        else:
            pltpu.make_async_copy(q_ref.at[:, src_cols(a)], qb.at[j, own_rows(a)], q_recv.at[j]).start()

            def one(da, _):
                a2 = lax.rem(a + da, A)
                remote(q_ref.at[:, src_cols(a2)], qb.at[j, own_rows(a)], q_send.at[j], q_recv.at[j], at(a2=a2)).start()
                return 0

            lax.fori_loop(1, A, one, 0)

    def first_text():
        pltpu.make_async_copy(t_ref.at[:, cols(a * width, width)], tb.at[slot, a], t_recv).start()

        def one(da, _):
            a2 = lax.rem(a + da, A)
            remote(t_ref.at[:, cols(a2 * width, width)], tb.at[slot, a], t_send, t_recv, at(a2=a2)).start()
            return 0

        lax.fori_loop(1, A, one, 0)

    first(0, "kv")
    first_text()
    first(0, "q")
    for j in range(1, hp):
        first(j, "kv")
        first(j, "q")

    weight_copies = []
    for j in range(hp):
        for b in range(X * A):
            weight_copies.append(
                pltpu.make_async_copy(
                    w_hbm.at[pl.ds((b * hp + j) * d, d)], wb.at[j, pl.ds(b * d, d)], w_sem.at[j]
                )
            )
            weight_copies[-1].start()

    def drain(ref, sem):
        pltpu.make_async_copy(ref, ref, sem).wait()

    def members():
        for dr in range(1, R):
            yield dr - 1, at(r2=lax.rem(r + dr, R))
        for dc in range(1, C):
            yield R - 2 + dc, at(c2=lax.rem(core + dc, C))

    def share(block, send, recv):
        for n, target in members():
            remote(block(slot), block(slot), send.at[n], recv.at[n], target).start()

    def forward(block, send, recv):
        base = R - 1 + C - 1
        for dr in range(1, R):
            from_slot = lax.rem(r - dr + R, R) * C + core
            drain(block(from_slot), recv.at[dr - 1])
            for dc in range(1, C):
                n = base + (dr - 1) * (C - 1) + dc - 1
                remote(
                    block(from_slot), block(from_slot), send.at[n], recv.at[n], at(c2=lax.rem(core + dc, C))
                ).start()

    def collect(block, recv):
        base = R - 1 + C - 1
        for dc in range(1, C):
            from_core = lax.rem(core - dc + C, C)
            drain(block(r * C + from_core), recv.at[R - 2 + dc])
            for dr in range(1, R):
                n = base + (dr - 1) * (C - 1) + dc - 1
                drain(block(lax.rem(r - dr + R, R) * C + from_core), recv.at[n])

    def shared_sends(block, send):
        for n in range(R - 1 + C - 1 + (R - 1) * (C - 1)):
            drain(block(slot), send.at[n])

    def kv_block(j):
        return lambda s: kv.at[j, :, s]

    def text_block(s):
        return tb.at[s]

    def share_kv(j):
        drain(kv.at[j, :, slot], kv_recv.at[j])
        share(kv_block(j), kv2_send.at[j], kv2_recv.at[j])

    def project(j):
        drain(att.at[j], o_recv.at[j])
        drain(wb.at[j], w_sem.at[j])
        columns = o_ref.shape[1]
        step = 768 if columns % 768 == 0 else d

        @pl.loop(0, columns // step)
        def _(i):
            part = pl.ds(pl.multiple_of(i * step, d), step)
            term = jnp.dot(att[j], wb[j, :, part], preferred_element_type=jnp.float32)
            if j > 0:
                term = acc[:, part] + term
            if j < hp - 1:
                acc[:, part] = term
            else:
                o_ref[:, part] = term.astype(o_ref.dtype)

    queries = qb.shape[1]
    tile = 128 if queries % 128 == 0 else rows
    scale = math.log2(math.e) * d ** (-0.5)
    nt = (((1,), (1,)), ((), ()))
    text = tkv.shape[2]

    share_kv(0)
    drain(tb.at[slot], t_recv)
    share(text_block, t2_send, t2_recv)
    for j in range(hp):
        forward(kv_block(j), kv2_send.at[j], kv2_recv.at[j])
        if j == 0:
            forward(text_block, t2_send, t2_recv)
            collect(text_block, t2_recv)
            block = tb[...].reshape(-1, width)
            for n in range(2):
                got = jnp.dot(pick_ref[n], block, preferred_element_type=jnp.float32).astype(jnp.bfloat16)
                for i in range(hp):
                    tkv[i, n] = got[:, i * d : (i + 1) * d]
        drain(qb.at[j], q_recv.at[j])
        collect(kv_block(j), kv2_recv.at[j])

        @pl.loop(0, queries // tile)
        def _(i):
            part = pl.ds(pl.multiple_of(i * tile, 16), tile)
            q = qb[j, part]
            keys = kv[j, 0].reshape(-1, d)
            values = kv[j, 1].reshape(-1, d)
            s1 = lax.dot_general(q, keys, nt, preferred_element_type=jnp.float32)
            s2 = lax.dot_general(q, tkv[j, 0], nt, preferred_element_type=jnp.float32)
            s2 = jnp.where(order_ref[...] < length_ref[0], s2, -1e30)
            top = jnp.maximum(jnp.max(s1, axis=1, keepdims=True), jnp.max(s2, axis=1, keepdims=True))
            p1 = jnp.exp2((s1 - top) * scale)
            p2 = jnp.exp2((s2 - top) * scale)
            total = jnp.sum(p1, axis=1, keepdims=True) + jnp.sum(p2, axis=1, keepdims=True)
            o = jnp.dot(p1.astype(jnp.bfloat16), values, preferred_element_type=jnp.float32)
            o = o + jnp.dot(p2.astype(jnp.bfloat16), tkv[j, 1], preferred_element_type=jnp.float32)
            ob[j, part] = (o / total).astype(jnp.bfloat16)

        column = cols((section * A + a) * d, d)
        pltpu.make_async_copy(ob.at[j, own_rows(a)], att.at[j, :, column], o_recv.at[j]).start()

        def back(da, _):
            a2 = lax.rem(a + da, A)
            for dx in range(X):
                remote(
                    ob.at[j, own_rows(a2)],
                    att.at[j, :, column],
                    o_send.at[j],
                    o_recv.at[j],
                    at(a2=a2, x2=lax.rem(section + dx, X)),
                ).start()
            return 0

        lax.fori_loop(1, A, back, 0)
        for dx in range(1, X):
            remote(
                ob.at[j, own_rows(a)],
                att.at[j, :, column],
                o_send.at[j],
                o_recv.at[j],
                at(x2=lax.rem(section + dx, X)),
            ).start()
        if j + 1 < hp:
            share_kv(j + 1)
        if j > 0:
            project(j - 1)
    project(hp - 1)

    for j in range(hp):
        if A > 1:
            drain(kv.at[j, :, slot, pl.ds(0, (A - 1) * rows)], kv_send.at[j])
            drain(qb.at[j, pl.ds(0, (A - 1) * rows)], q_send.at[j])
        if A * X > 1:
            drain(att.at[j, :, pl.ds(0, (A * X - 1) * d)], o_send.at[j])
        shared_sends(kv_block(j), kv2_send.at[j])
    if A > 1:
        drain(tb.at[slot, pl.ds(0, A - 1)], t_send)
    shared_sends(text_block, t2_send)


def shards(sizes, queries, keys, values, text_keys, text_values, text_length, out_weight):
    S, C, X = sizes
    rows, columns = queries.shape
    heads = columns // HEAD_DIM
    A = math.gcd(heads, S)
    R = S // A
    hp = heads // A
    text_rows = text_keys.shape[0]
    text = text_rows * S * C
    bf16 = jnp.bfloat16
    packed = jnp.concatenate(
        [text_keys, text_values, jnp.zeros((PAD - 2 * text_rows, columns), bf16)], axis=0
    )
    t = np.arange(text)
    block, i = t // text_rows, t % text_rows
    from_slot, from_a = block // A, block % A
    from_r, from_c = from_slot // C, from_slot % C
    order = (((from_a * R + from_r) * C + from_c) * text_rows + i).astype(np.int32)[None, :]
    pick = np.zeros((2, text, R * C * A * PAD), np.float32)
    for n in range(2):
        pick[n, t, block * PAD + n * text_rows + i] = 1.0
    pick = jnp.asarray(pick, bf16)
    out_columns = out_weight.shape[1]
    shares = R - 1 + C - 1 + (R - 1) * (C - 1)
    vmem = pl.BlockSpec(memory_space=pltpu.VMEM)
    dma = pltpu.SemaphoreType.DMA
    return pl.pallas_call(
        functools.partial(kernel, (A, R, C, X, hp)),
        out_shape=jax.ShapeDtypeStruct((rows, out_columns), bf16),
        in_specs=[pl.BlockSpec(memory_space=pltpu.SMEM)] + [vmem] * 6 + [pl.BlockSpec(memory_space=pl.ANY)],
        out_specs=vmem,
        scratch_shapes=[
            pltpu.VMEM((hp, A * rows, HEAD_DIM), bf16),
            pltpu.VMEM((hp, 2, R * C, A * rows, HEAD_DIM), bf16),
            pltpu.VMEM((R * C, A, PAD, hp * HEAD_DIM), bf16),
            pltpu.VMEM((hp, 2, text, HEAD_DIM), bf16),
            pltpu.VMEM((hp, A * rows, HEAD_DIM), bf16),
            pltpu.VMEM((hp, rows, X * A * HEAD_DIM), bf16),
            pltpu.VMEM((hp, X * A * HEAD_DIM, out_columns), bf16),
            pltpu.VMEM((rows, out_columns), jnp.float32),
            dma,
            dma((hp,)),
            dma((hp,)),
            dma((hp,)),
            dma,
            dma((hp,)),
            dma((hp,)),
            dma((hp,)),
            dma,
            dma((hp,)),
            dma((hp, shares)),
            dma((hp, shares)),
            dma((shares,)),
            dma((shares,)),
        ],
        compiler_params=pltpu.CompilerParams(
            collective_id=0, has_side_effects=True, vmem_limit_bytes=60 * 1024 * 1024
        ),
    )(text_length, queries, keys, values, packed, jnp.asarray(order), pick, out_weight)


def solution(mesh):
    sizes = (mesh.shape["seq"], mesh.shape["head"], mesh.shape["section"])
    tokens = P(("groups", "seq", "head"), "section")
    return jax.shard_map(
        functools.partial(shards, sizes),
        mesh=mesh,
        in_specs=(tokens,) * 5 + (P("groups"), P(None, "section")),
        out_specs=tokens,
        check_vma=False,
    )
```

time: 290 us -> 76.6 us (0.26)
  blocking collectives: 108 us -> 0 us
  waiting for transfers between devices: 87.4 us -> 0 us
  Pallas kernels: 0 us -> 72 us
  matrix products: 37.1 us -> 0 us
  local copies, waits for them, and re-layouts: 27.4 us -> 1.92 us
  between operations: 14.2 us -> 0.67 us
  other arithmetic: 10.8 us -> 1.48 us
  starting transfers between devices: 3.91 us -> 0 us
    all_gather x2 -> x0, blocking collectives: 92.2 us -> none  [the longest x1 49.3 us: shards(): lax.all_gather(text_values, ('seq', 'head'), axis=0, tiled=True)]
    all_gather x2 -> x0, waiting for transfers between devices: 86.1 us -> none  [the longest x1 76.6 us: shards(): lax.all_gather(local_v, 'seq', axis=0, tiled=True)]
    pallas_call x0 -> x1, Pallas kernels: none -> 72 us  [shards(): pl.pallas_call(functools.partial(kernel, (A, R, C, X, hp)), out_shape=jax...]
    dot_general x5 -> x0, matrix products: 37.1 us -> none  [the longest x2 13.7 us: absorb(): jnp.einsum('qhd,khd->qhk', queries_heads, keys_heads, preferred_element_t...]
    all_gather x2 -> x0, local copies, waits for them, and re-layouts: 21.7 us -> none  [the longest x1 10.8 us: shards(): lax.all_gather(local_k, 'seq', axis=0, tiled=True)]
    all_to_all x3 -> x0, blocking collectives: 15.5 us -> none  [the longest x1 6.08 us: shards(): lax.all_to_all(finish(running), 'head', split_axis=0, concat_axis=1, tile...]
    reduce_sum x2 -> x0, other arithmetic: 10.8 us -> none  [absorb(): totals = totals * factor + jnp.sum(weights, axis=-1)]
    all_to_all x4 -> x0, local copies, waits for them, and re-layouts: 4 us -> none  [the longest x1 1.84 us: shards(): lax.all_to_all(queries, 'head', split_axis=1, concat_axis=0, tiled=True)]
  transfers between devices with their start and end apart: 3 -> 0, of which waited for: 3 -> 0; matrix products, arithmetic and copies ran while one was open for 13% -> 0% of each run, Pallas kernels for 0% -> 0%
where the time goes in v1:
time: 76.6 us; the launch traced here: 76.1 us
  Pallas kernels  72 us (94%)
  local copies, waits for them, and re-layouts  1.92 us (3%)
  other arithmetic  1.48 us (2%)
    pallas_call x1, Pallas kernels, shards(): pl.pallas_call(functools.partial(kernel, (A, R, C, X, hp)), out_shape=jax...  72 us
    unnamed x1, local copies, waits for them, and re-layouts  1.84 us

profile of v1, /device:TPU:1, one launch (start us, length us, event | category | flops | bytes accessed | tf_op | source)
XLA Modules:
  0.0 76.1 jit_solution(14444496095457874937)
XLA Ops:
  0.7 0.1 pad.2.clone
  0.7 1.5 %maximum_maximum_fusion.t_ref = bf16[16,3072]{1,0:T(8,128)(2,1)} fusion(bf16[4,3072]{1,0:T(4,128)(2,1)} %param.13, bf16[4,3072]{1,0:T(4,128)(2,1)} %param.12, bf16[16]{0:T(256)(128)(2,1)S(1)} %pad.2.clone), kind=kLoop, calls=%fused_computation | loop fusion | flops 294912 | bytes 147488 | tf_op jit(solution)/shard_map/concatenate | solution.py:303
  2.2 72.0 %shard_map.91 = bf16[80,3072]{1,0:T(8,128)(2,1)} custom-call(s32[1]{0:T(128)S(6)} %copy.11.length_ref, bf16[80,3072]{1,0:T(8,128)(2,1)} %q_ref.1, bf16[80,3072]{1,0:T(8,128)(2,1)} %k_ref.1, bf16[80,3072]{1,0:T(8,128)(2,1)} %v_ref.1, bf16[16,3072]{1,0:T(8,128)(2,1)} %maximum_maximum_fusion.t_ref, s32[1,128]{1,0:T(1,128)} %constant.7.clone.order_ref, ...), custom_call_target="tpu_custom_call" | custom-call | tf_op jit(solution)/shard_map/pallas_call | solution.py:319
  74.2 1.8 %copy.12 = bf16[80,3072]{1,0:T(8,128)(2,1)} copy(bf16[80,3072]{1,0:T(8,128)(2,1)} %shard_map.91) | data formatting | bytes 983040
  (1 shorter events, 0.0 us)

commit v2 on v1

v2 whole, which is shorter than its diff:
```python
import functools
import math

import jax
import jax.numpy as jnp
import numpy as np
from jax import lax
from jax.experimental import pallas as pl
from jax.experimental.pallas import tpu as pltpu
from jax.sharding import PartitionSpec as P

HEAD_DIM = 128
MESH = pl.DeviceIdType.MESH


def kernel(
    dims,
    length_ref,
    q_ref,
    k_ref,
    v_ref,
    t_ref,
    order_ref,
    pick_hbm,
    w_hbm,
    o_ref,
    qb,
    kv,
    tb,
    tkv,
    ob,
    att,
    wb,
    acc,
    pick_ref,
    local_sem,
    w_sem,
    q_send,
    kv_send,
    t_send,
    o_send,
    q_recv,
    kv_recv,
    t_recv,
    o_recv,
    kv2_send,
    kv2_recv,
    t2_send,
    t2_recv,
):
    A, R, C, X, hp = dims
    d = HEAD_DIM
    rows = q_ref.shape[0]
    seq = lax.axis_index("seq")
    core = lax.axis_index("head")
    section = lax.axis_index("section")
    a = seq // R
    r = lax.rem(seq, R)
    slot = r * C + core
    width = hp * d

    def at(a2=None, r2=None, c2=None, x2=None):
        return {
            "seq": (a if a2 is None else a2) * R + (r if r2 is None else r2),
            "head": core if c2 is None else c2,
            "section": section if x2 is None else x2,
        }

    def cols(start, size):
        return pl.ds(pl.multiple_of(start, d), size)

    def own_rows(which):
        return pl.ds(pl.multiple_of(which * rows, 16), rows)

    barrier = pltpu.get_barrier_semaphore()

    def greet(target):
        pl.semaphore_signal(barrier, inc=1, device_id=target, device_id_type=MESH)

    for da in range(A):
        for dx in range(X):
            if da or dx:
                greet(at(a2=lax.rem(a + da, A), x2=lax.rem(section + dx, X)))
    for dr in range(1, R):
        greet(at(r2=lax.rem(r + dr, R)))
    for dc in range(1, C):
        greet(at(c2=lax.rem(core + dc, C)))
    pl.semaphore_wait(barrier, A * X - 1 + R - 1 + C - 1)

    def remote(src, dst, send, recv, target):
        return pltpu.make_async_remote_copy(
            src_ref=src, dst_ref=dst, send_sem=send, recv_sem=recv, device_id=target, device_id_type=MESH
        )

    def first(j, ref, landing, send, recv):
        src_cols = lambda a2: cols((a2 * hp + j) * d, d)
        pltpu.make_async_copy(ref.at[:, src_cols(a)], landing.at[own_rows(a)], recv).start()

        def one(da, _):
            a2 = lax.rem(a + da, A)
            remote(ref.at[:, src_cols(a2)], landing.at[own_rows(a)], send, recv, at(a2=a2)).start()
            return 0

        lax.fori_loop(1, A, one, 0)

    def first_kv(j, n):
        first(j, (k_ref, v_ref)[n], kv.at[j, n, slot], kv_send.at[j, n], kv_recv.at[j, n])

    def first_q(j):
        first(j, q_ref, qb.at[j], q_send.at[j], q_recv.at[j])

    def first_text():
        pltpu.make_async_copy(t_ref.at[:, cols(a * width, width)], tb.at[slot, a], t_recv).start()

        def one(da, _):
            a2 = lax.rem(a + da, A)
            remote(t_ref.at[:, cols(a2 * width, width)], tb.at[slot, a], t_send, t_recv, at(a2=a2)).start()
            return 0

        lax.fori_loop(1, A, one, 0)

    for j in range(hp):
        first_kv(j, 0)
        first_kv(j, 1)
        if j == 0:
            first_text()
    for j in range(hp):
        first_q(j)

    pick_copy = pltpu.make_async_copy(pick_hbm, pick_ref, local_sem)
    pick_copy.start()

    weight_copies = []
    for j in range(hp):
        for b in range(X * A):
            weight_copies.append(
                pltpu.make_async_copy(
                    w_hbm.at[pl.ds((b * hp + j) * d, d)], wb.at[j, pl.ds(b * d, d)], w_sem.at[j]
                )
            )
            weight_copies[-1].start()

    def drain(ref, sem):
        pltpu.make_async_copy(ref, ref, sem).wait()

    def members():
        for dr in range(1, R):
            yield dr - 1, at(r2=lax.rem(r + dr, R))
        for dc in range(1, C):
            yield R - 2 + dc, at(c2=lax.rem(core + dc, C))

    def share(block, send, recv):
        for n, target in members():
            remote(block(slot), block(slot), send.at[n], recv.at[n], target).start()

    def forward(block, send, recv):
        base = R - 1 + C - 1
        for dr in range(1, R):
            from_slot = lax.rem(r - dr + R, R) * C + core
            drain(block(from_slot), recv.at[dr - 1])
            for dc in range(1, C):
                n = base + (dr - 1) * (C - 1) + dc - 1
                remote(
                    block(from_slot), block(from_slot), send.at[n], recv.at[n], at(c2=lax.rem(core + dc, C))
                ).start()

    def collect(block, recv):
        base = R - 1 + C - 1
        for dc in range(1, C):
            from_core = lax.rem(core - dc + C, C)
            drain(block(r * C + from_core), recv.at[R - 2 + dc])
            for dr in range(1, R):
                n = base + (dr - 1) * (C - 1) + dc - 1
                drain(block(lax.rem(r - dr + R, R) * C + from_core), recv.at[n])

    def shared_sends(block, send):
        for n in range(R - 1 + C - 1 + (R - 1) * (C - 1)):
            drain(block(slot), send.at[n])

    def kv_block(j, n):
        return lambda s: kv.at[j, n, s]

    def text_block(s):
        return tb.at[s]

    def share_kv(j):
        for n in range(2):
            drain(kv.at[j, n, slot], kv_recv.at[j, n])
            share(kv_block(j, n), kv2_send.at[j, n], kv2_recv.at[j, n])

    def project(j):
        drain(att.at[j], o_recv.at[j])
        drain(wb.at[j], w_sem.at[j])
        columns = o_ref.shape[1]
        step = 768 if columns % 768 == 0 else d

        @pl.loop(0, columns // step)
        def _(i):
            part = pl.ds(pl.multiple_of(i * step, d), step)
            term = jnp.dot(att[j], wb[j, :, part], preferred_element_type=jnp.float32)
            if j > 0:
                term = acc[:, part] + term
            if j < hp - 1:
                acc[:, part] = term
            else:
                o_ref[:, part] = term.astype(o_ref.dtype)

    group = 2 if A % 2 == 0 else 1
    tile = group * rows
    scale = math.log2(math.e) * d ** (-0.5)
    nt = (((1,), (1,)), ((), ()))

    def attend(j, i):
        part = pl.ds(pl.multiple_of(i * tile, 16), tile)
        q = qb[j, part]
        keys = kv[j, 0].reshape(-1, d)
        values = kv[j, 1].reshape(-1, d)
        s1 = lax.dot_general(q, keys, nt, preferred_element_type=jnp.float32)
        s2 = lax.dot_general(q, tkv[j, 0], nt, preferred_element_type=jnp.float32)
        s2 = jnp.where(order_ref[...] < length_ref[0], s2, -1e30)
        top = jnp.maximum(jnp.max(s1, axis=1, keepdims=True), jnp.max(s2, axis=1, keepdims=True))
        p1 = jnp.exp2((s1 - top) * scale)
        p2 = jnp.exp2((s2 - top) * scale)
        total = jnp.sum(p1, axis=1, keepdims=True) + jnp.sum(p2, axis=1, keepdims=True)
        o = jnp.dot(p1.astype(jnp.bfloat16), values, preferred_element_type=jnp.float32)
        o = o + jnp.dot(p2.astype(jnp.bfloat16), tkv[j, 1], preferred_element_type=jnp.float32)
        ob[j, part] = (o / total).astype(jnp.bfloat16)

    column = cols((section * A + a) * d, d)

    def back(j, a2, dx):
        remote(
            ob.at[j, own_rows(a2)],
            att.at[j, :, column],
            o_send.at[j],
            o_recv.at[j],
            at(a2=a2, x2=lax.rem(section + dx, X)),
        ).start()

    def back_group(j, i):
        for b in range(group):
            for dx in range(X):
                back(j, i * group + b, dx)

    def back_own(j, i):
        for b in range(group):
            for dx in range(1, X):
                back(j, i * group + b, dx)
            if group > 1:
                @pl.when(i * group + b != a)
                def _():
                    back(j, i * group + b, 0)
        pltpu.make_async_copy(ob.at[j, own_rows(a)], att.at[j, :, column], o_recv.at[j]).start()

    own = a // group
    groups = A // group

    def attention(j):
        @pl.loop(1, groups)
        def _(di):
            i = lax.rem(own + di, groups)
            attend(j, i)
            back_group(j, i)

        attend(j, own)
        back_own(j, own)

    def forward_kv(j):
        for n in range(2):
            forward(kv_block(j, n), kv2_send.at[j, n], kv2_recv.at[j, n])

    share_kv(0)
    drain(tb.at[slot], t_recv)
    share(text_block, t2_send, t2_recv)
    for j in range(1, hp):
        share_kv(j)
        forward_kv(j - 1)
        if j == 1:
            forward(text_block, t2_send, t2_recv)
    if hp == 1:
        forward(text_block, t2_send, t2_recv)
    collect(text_block, t2_recv)
    pick_copy.wait()
    block = tb[...].reshape(-1, width)
    for n in range(2):
        got = jnp.dot(pick_ref[n], block, preferred_element_type=jnp.float32).astype(jnp.bfloat16)
        for i in range(hp):
            tkv[i, n] = got[:, i * d : (i + 1) * d]
    for j in range(hp):
        if j == hp - 1:
            forward_kv(j)
        drain(qb.at[j], q_recv.at[j])
        for n in range(2):
            collect(kv_block(j, n), kv2_recv.at[j, n])
        attention(j)
    for j in range(hp):
        project(j)

    for j in range(hp):
        for n in range(2):
            if A > 1:
                drain(kv.at[j, n, slot, pl.ds(0, (A - 1) * rows)], kv_send.at[j, n])
            shared_sends(kv_block(j, n), kv2_send.at[j, n])
        if A > 1:
            drain(qb.at[j, pl.ds(0, (A - 1) * rows)], q_send.at[j])
        if A * X > 1:
            drain(att.at[j, :, pl.ds(0, (A * X - 1) * d)], o_send.at[j])
    if A > 1:
        drain(tb.at[slot, pl.ds(0, A - 1)], t_send)
    shared_sends(text_block, t2_send)


def shards(sizes, queries, keys, values, text_keys, text_values, text_length, out_weight):
    S, C, X = sizes
    rows, columns = queries.shape
    heads = columns // HEAD_DIM
    A = math.gcd(heads, S)
    R = S // A
    hp = heads // A
    text_rows = text_keys.shape[0]
    text = text_rows * S * C
    bf16 = jnp.bfloat16
    pad = -(-2 * text_rows // 8) * 8
    packed = jnp.concatenate([text_keys, text_values], axis=0)
    packed = jnp.pad(packed, ((0, pad - 2 * text_rows), (0, 0)))
    t = np.arange(text)
    block, i = t // text_rows, t % text_rows
    from_slot, from_a = block // A, block % A
    from_r, from_c = from_slot // C, from_slot % C
    order = (((from_a * R + from_r) * C + from_c) * text_rows + i).astype(np.int32)[None, :]
    pick = np.zeros((2, text, R * C * A * pad), np.float32)
    for n in range(2):
        pick[n, t, block * pad + n * text_rows + i] = 1.0
    pick = jnp.asarray(pick, bf16)
    out_columns = out_weight.shape[1]
    shares = R - 1 + C - 1 + (R - 1) * (C - 1)
    vmem = pl.BlockSpec(memory_space=pltpu.VMEM)
    hbm = pl.BlockSpec(memory_space=pl.ANY)
    dma = pltpu.SemaphoreType.DMA
    return pl.pallas_call(
        functools.partial(kernel, (A, R, C, X, hp)),
        out_shape=jax.ShapeDtypeStruct((rows, out_columns), bf16),
        in_specs=[pl.BlockSpec(memory_space=pltpu.SMEM)] + [hbm] * 4 + [vmem] + [hbm] * 2,
        out_specs=vmem,
        scratch_shapes=[
            pltpu.VMEM((hp, A * rows, HEAD_DIM), bf16),
            pltpu.VMEM((hp, 2, R * C, A * rows, HEAD_DIM), bf16),
            pltpu.VMEM((R * C, A, pad, hp * HEAD_DIM), bf16),
            pltpu.VMEM((hp, 2, text, HEAD_DIM), bf16),
            pltpu.VMEM((hp, A * rows, HEAD_DIM), bf16),
            pltpu.VMEM((hp, rows, X * A * HEAD_DIM), bf16),
            pltpu.VMEM((hp, X * A * HEAD_DIM, out_columns), bf16),
            pltpu.VMEM((rows, out_columns), jnp.float32),
            pltpu.VMEM(pick.shape, bf16),
            dma,
            dma((hp,)),
            dma((hp,)),
            dma((hp, 2)),
            dma,
            dma((hp,)),
            dma((hp,)),
            dma((hp, 2)),
            dma,
            dma((hp,)),
            dma((hp, 2, shares)),
            dma((hp, 2, shares)),
            dma((shares,)),
            dma((shares,)),
        ],
        compiler_params=pltpu.CompilerParams(
            collective_id=0, has_side_effects=True, vmem_limit_bytes=60 * 1024 * 1024
        ),
    )(text_length, queries, keys, values, packed, jnp.asarray(order), pick, out_weight)


def solution(mesh):
    sizes = (mesh.shape["seq"], mesh.shape["head"], mesh.shape["section"])
    tokens = P(("groups", "seq", "head"), "section")
    return jax.shard_map(
        functools.partial(shards, sizes),
        mesh=mesh,
        in_specs=(tokens,) * 5 + (P("groups"), P(None, "section")),
        out_specs=tokens,
        check_vma=False,
    )
```

time: 76.6 us -> 60.7 us (0.79)
  Pallas kernels: 72 us -> 56.6 us
    pallas_call x1, Pallas kernels: 72 us -> 56.6 us  [shards(): pl.pallas_call(functools.partial(kernel, (A, R, C, X, hp)), out_shape=jax...]
where the time goes in v2:
time: 60.7 us; the launch traced here: 60.5 us
  Pallas kernels  56.6 us (93%)
  local copies, waits for them, and re-layouts  1.84 us (3%)
  other arithmetic  1.4 us (2%)
  between operations  0.66 us (1%)
    pallas_call x1, Pallas kernels, shards(): pl.pallas_call(functools.partial(kernel, (A, R, C, X, hp)), out_shape=jax...  56.6 us
    unnamed x1, local copies, waits for them, and re-layouts  1.84 us
    concatenate x1, other arithmetic, shards(): packed = jnp.concatenate([text_keys, text_values], axis=0)  1.4 us

profile of v2, /device:TPU:1, one launch (start us, length us, event | category | flops | bytes accessed | tf_op | source)
XLA Modules:
  0.0 60.5 jit_solution(16589801781154267256)
XLA Ops:
  0.7 1.4 %pad_maximum_fusion.t_ref = bf16[8,3072]{1,0:T(8,128)(2,1)} fusion(bf16[4,3072]{1,0:T(4,128)(2,1)} %param.13, bf16[4,3072]{1,0:T(4,128)(2,1)} %param.12), kind=kLoop, calls=%fused_computation | loop fusion | flops 98304 | bytes 98304 | tf_op jit(solution)/shard_map/concatenate | solution.py:324
  2.1 56.6 %shard_map.91 = bf16[80,3072]{1,0:T(8,128)(2,1)} custom-call(s32[1]{0:T(128)S(6)} %copy.11.length_ref, bf16[80,3072]{1,0:T(8,128)(2,1)} %q_ref.1, bf16[80,3072]{1,0:T(8,128)(2,1)} %k_ref.1, bf16[80,3072]{1,0:T(8,128)(2,1)} %v_ref.1, bf16[8,3072]{1,0:T(8,128)(2,1)} %pad_maximum_fusion.t_ref, s32[1,128]{1,0:T(1,128)} %constant.6.clone.order_ref, ...), custom_call_target="tpu_custom_call" | custom-call | tf_op jit(solution)/shard_map/pallas_call | solution.py:340
  58.6 1.8 %copy.12 = bf16[80,3072]{1,0:T(8,128)(2,1)} copy(bf16[80,3072]{1,0:T(8,128)(2,1)} %shard_map.91) | data formatting | bytes 983040

commit v3 on v2

--- a/solution.py
+++ b/solution.py
@@ -19,11 +19,12 @@
     q_ref,
     k_ref,
     v_ref,
-    t_ref,
+    tk_ref,
+    tv_ref,
     order_ref,
     pick_hbm,
     w_hbm,
-    o_ref,
+    o_out,
     qb,
     kv,
     tb,
@@ -33,6 +34,10 @@
     wb,
     acc,
     pick_ref,
+    o_ref,
+    wide,
+    packed,
+    t_ref,
     local_sem,
     w_sem,
     q_send,
@@ -110,6 +115,13 @@
         first(j, q_ref, qb.at[j], q_send.at[j], q_recv.at[j])
 
     def first_text():
+        count = tk_ref.shape[0]
+        if 2 * count < wide.shape[0]:
+            wide[...] = jnp.zeros_like(wide)
+        wide[:count] = tk_ref[...].astype(jnp.float32)
+        wide[count : 2 * count] = tv_ref[...].astype(jnp.float32)
+        packed[...] = wide[...].astype(jnp.bfloat16)
+        pltpu.sync_copy(packed, t_ref)
         pltpu.make_async_copy(t_ref.at[:, cols(a * width, width)], tb.at[slot, a], t_recv).start()
 
         def one(da, _):
@@ -295,6 +307,8 @@
         attention(j)
     for j in range(hp):
         project(j)
+    out_copy = pltpu.make_async_copy(o_ref, o_out, local_sem)
+    out_copy.start()
 
     for j in range(hp):
         for n in range(2):
@@ -308,6 +322,7 @@
     if A > 1:
         drain(tb.at[slot, pl.ds(0, A - 1)], t_send)
     shared_sends(text_block, t2_send)
+    out_copy.wait()
 
 
 def shards(sizes, queries, keys, values, text_keys, text_values, text_length, out_weight):
@@ -321,8 +336,6 @@
     text = text_rows * S * C
     bf16 = jnp.bfloat16
     pad = -(-2 * text_rows // 8) * 8
-    packed = jnp.concatenate([text_keys, text_values], axis=0)
-    packed = jnp.pad(packed, ((0, pad - 2 * text_rows), (0, 0)))
     t = np.arange(text)
     block, i = t // text_rows, t % text_rows
     from_slot, from_a = block // A, block % A
@@ -340,8 +353,8 @@
     return pl.pallas_call(
         functools.partial(kernel, (A, R, C, X, hp)),
         out_shape=jax.ShapeDtypeStruct((rows, out_columns), bf16),
-        in_specs=[pl.BlockSpec(memory_space=pltpu.SMEM)] + [hbm] * 4 + [vmem] + [hbm] * 2,
-        out_specs=vmem,
+        in_specs=[pl.BlockSpec(memory_space=pltpu.SMEM)] + [hbm] * 3 + [vmem] * 3 + [hbm] * 2,
+        out_specs=pl.BlockSpec(memory_space=pl.ANY),
         scratch_shapes=[
             pltpu.VMEM((hp, A * rows, HEAD_DIM), bf16),
             pltpu.VMEM((hp, 2, R * C, A * rows, HEAD_DIM), bf16),
@@ -352,6 +365,10 @@
             pltpu.VMEM((hp, X * A * HEAD_DIM, out_columns), bf16),
             pltpu.VMEM((rows, out_columns), jnp.float32),
             pltpu.VMEM(pick.shape, bf16),
+            pltpu.VMEM((rows, out_columns), bf16),
+            pltpu.VMEM((pad, columns), jnp.float32),
+            pltpu.VMEM((pad, columns), bf16),
+            pltpu.VMEM((pad, columns), bf16),
             dma,
             dma((hp,)),
             dma((hp,)),
@@ -370,7 +387,7 @@
         compiler_params=pltpu.CompilerParams(
             collective_id=0, has_side_effects=True, vmem_limit_bytes=60 * 1024 * 1024
         ),
-    )(text_length, queries, keys, values, packed, jnp.asarray(order), pick, out_weight)
+    )(text_length, queries, keys, values, text_keys, text_values, jnp.asarray(order), pick, out_weight)
 
 
 def solution(mesh):

time: 60.7 us -> 59.4 us (0.979)
  other arithmetic: 1.4 us -> 0 us
    concatenate x1 -> x0, other arithmetic: 1.4 us -> none  [shards(): packed = jnp.concatenate([text_keys, text_values], axis=0)]
where the time goes in v3:
time: 59.4 us; the launch traced here: 59.1 us
  Pallas kernels  56.6 us (95%)
  local copies, waits for them, and re-layouts  1.84 us (3%)
  between operations  0.66 us (1%)
    pallas_call x1, Pallas kernels, shards(): pl.pallas_call(functools.partial(kernel, (A, R, C, X, hp)), out_shape=jax...  56.6 us
    unnamed x1, local copies, waits for them, and re-layouts  1.84 us

profile of v3, /device:TPU:1, one launch (start us, length us, event | category | flops | bytes accessed | tf_op | source)
XLA Modules:
  0.0 59.1 jit_solution(8117533461643635574)
XLA Ops:
  0.7 56.6 %shard_map.91 = bf16[80,3072]{1,0:T(8,128)(2,1)} custom-call(s32[1]{0:T(128)S(6)} %copy.11.length_ref, bf16[80,3072]{1,0:T(8,128)(2,1)} %q_ref.1, bf16[80,3072]{1,0:T(8,128)(2,1)} %k_ref.1, bf16[80,3072]{1,0:T(8,128)(2,1)} %v_ref.1, bf16[4,3072]{1,0:T(4,128)(2,1)} %tk_ref.1, bf16[4,3072]{1,0:T(4,128)(2,1)} %tv_ref.1, s32[1,128]{1,0:T(1,128)} %constant.5.clone.order_ref, ...), custom_call_target="tpu_custom_call" | custom-call | tf_op jit(solution)/shard_map/pallas_call | solution.py:353
  57.3 1.8 %copy.12 = bf16[80,3072]{1,0:T(8,128)(2,1)} copy(bf16[80,3072]{1,0:T(8,128)(2,1)} %shard_map.91) | data formatting | bytes 983040

commit v4 on v3

--- a/solution.py
+++ b/solution.py
@@ -217,7 +217,7 @@
             else:
                 o_ref[:, part] = term.astype(o_ref.dtype)
 
-    group = 2 if A % 2 == 0 else 1
+    group = 1
     tile = group * rows
     scale = math.log2(math.e) * d ** (-0.5)
     nt = (((1,), (1,)), ((), ()))

time: 59.4 us -> 66.2 us (1.11)
  Pallas kernels: 56.6 us -> 63.5 us
    pallas_call x1, Pallas kernels: 56.6 us -> 63.5 us  [shards(): pl.pallas_call(functools.partial(kernel, (A, R, C, X, hp)), out_shape=jax...]
where the time goes in v4:
time: 66.2 us; the launch traced here: 66 us
  Pallas kernels  63.5 us (96%)
  local copies, waits for them, and re-layouts  1.84 us (3%)
    pallas_call x1, Pallas kernels, shards(): pl.pallas_call(functools.partial(kernel, (A, R, C, X, hp)), out_shape=jax...  63.5 us
    unnamed x1, local copies, waits for them, and re-layouts  1.84 us

profile of v4, /device:TPU:1, one launch (start us, length us, event | category | flops | bytes accessed | tf_op | source)
XLA Modules:
  0.0 66.0 jit_solution(17253183084038874753)
XLA Ops:
  0.7 63.5 %shard_map.91 = bf16[80,3072]{1,0:T(8,128)(2,1)} custom-call(s32[1]{0:T(128)S(6)} %copy.11.length_ref, bf16[80,3072]{1,0:T(8,128)(2,1)} %q_ref.1, bf16[80,3072]{1,0:T(8,128)(2,1)} %k_ref.1, bf16[80,3072]{1,0:T(8,128)(2,1)} %v_ref.1, bf16[4,3072]{1,0:T(4,128)(2,1)} %tk_ref.1, bf16[4,3072]{1,0:T(4,128)(2,1)} %tv_ref.1, s32[1,128]{1,0:T(1,128)} %constant.5.clone.order_ref, ...), custom_call_target="tpu_custom_call" | custom-call | tf_op jit(solution)/shard_map/pallas_call | solution.py:353
  64.2 1.8 %copy.12 = bf16[80,3072]{1,0:T(8,128)(2,1)} copy(bf16[80,3072]{1,0:T(8,128)(2,1)} %shard_map.91) | data formatting | bytes 983040
